TPU v7x, 32 devices: a whole 2x2x4 slice. The times are simulated.
32 devices in a mesh: wave: 4 (over z), tile: 8 (over y, x, core).
Axes of the slice: x: 2, y: 2, z: 4, core: 2. Of those that a mesh axis runs over, the one named last changes fastest.
Arguments:
- initial_fields: bfloat16 [16, 8, 256, 1024], P('wave', None, 'tile'), may hold values from -6 to 6
- conductivity: float32 [256, 1024], P('tile'), may hold values from 0.1 to 10
- wavenumbers: float32 [16], replicated, may hold values from 0.05 to 1.5
- quad_weights: float32 [16], replicated, may hold values from 0.05 to 0.3
- sweep_counts: int32 [16], replicated, may hold values from 1 to 8, as said below
- electrode_cells: int32 [64], replicated, may hold values from 0 to 255
- source_pairs: int32 [8, 2], replicated, may hold values from 0 to 63, as said below
Outputs:
- potential: float32 [8, 256, 1024], P('wave', 'tile')
Inputs may be any that keep to these rules, and one draw needn't show every extreme that they name: `sweep_counts`: each wavenumber gets at least one sweep and at most 8. `source_pairs`: the two electrodes of a source column are different electrodes.
All inputs are finite; a program needn't handle non-finite values.
Results may differ from a plain program's by a relative error of at most 0.0003.
Values may be sent and summed in bfloat16 or wider, within the bound.
No kernel may reach another device: no remote copies, remote signals or barrier semaphores. Data moves between devices by JAX's collectives and lax.ppermute only.
A program may use at most 64 MiB of HBM per device.

v0:
```python
import functools

import jax
import jax.numpy as jnp
from jax import lax
from jax.experimental import pallas as pl
from jax.experimental.pallas import tpu as pltpu
from jax.sharding import PartitionSpec as P


ITERS = 8
LOWER = 0.1
UPPER = 2.0
THETA = (UPPER + LOWER) / 2.0
DELTA = (UPPER - LOWER) / 2.0
SIGMA_ONE = THETA / DELTA
CURRENT = 2.0
DIAG = 2.0 * (THETA - 1.0) / DELTA
LANES = 128
SUB = 8
UNROLL = 4
PLANES = 3


def chebyshev_table():
    values = [1.0, SIGMA_ONE]
    for _ in range(ITERS):
        values.append(2.0 * SIGMA_ONE * values[-1] - values[-2])
    return values


TABLE = chebyshev_table()


def pick(values, t):
    result = jnp.float32(values[0])
    for k in range(1, len(values)):
        result = jnp.where(t == k, jnp.float32(values[k]), result)
    return result


def exchange(values, lanes):
    values = list(values)
    step = len(values) // 2
    while step:
        upper = lax.rem(lax.div(lanes, step), 2) == 1
        for i in range(len(values)):
            if i & step:
                continue
            low, high = values[i], values[i + step]
            values[i] = jnp.where(upper, pltpu.roll(high, step, 1), low)
            values[i + step] = jnp.where(upper, high, pltpu.roll(low, LANES - step, 1))
        step //= 2
    return values


def wrap_west(value, lanes, span):
    return jnp.take_along_axis(
        value, jnp.where(lanes < span, lanes + (LANES - span - 1), lanes - span), axis=1,
        mode="promise_in_bounds",
    )


def wrap_east(value, lanes, span):
    return jnp.take_along_axis(
        value, jnp.where(lanes < LANES - span, lanes + span, lanes - (LANES - span - 1)), axis=1,
        mode="promise_in_bounds",
    )


def pieces(value):
    return [value[:, j:j + LANES] for j in range(0, value.shape[1], LANES)]


def coefficients_kernel(
    wavenumbers, near, cond, across,
    c_north, c_east, c_wrap, root, inverse, q_first, cond_pad, q_pad,
):
    rows, _ = cond.shape
    halo = near.shape[1]
    waves, width = root.shape[:2]
    tall = rows + 2 * halo
    pair = SUB // waves
    first = lax.axis_index("wave") * waves
    lanes = lax.broadcasted_iota(jnp.int32, (SUB, LANES), 1)
    squares = [wavenumbers[first + w] * wavenumbers[first + w] for w in range(waves)]
    blank = jnp.zeros((SUB, LANES), jnp.float32)

    def store(at, value):
        for j, part in enumerate(exchange(pieces(value), lanes)):
            cond_pad[j, pl.ds(at, SUB), :] = part

    for j in range(width):
        cond_pad[j, pl.ds(0, SUB), :] = blank
        cond_pad[j, pl.ds(SUB + tall, SUB), :] = blank
        for w in range(waves):
            q_pad[w, j, pl.ds(0, SUB), :] = blank
    low = lax.rem(lax.axis_index("tile"), 2) == 0
    for ref, at in (
        (near, jnp.where(low, SUB + halo + rows, SUB)),
        (across, jnp.where(low, SUB, SUB + halo + rows)),
    ):
        planes = [ref[SUB + i].astype(jnp.float32) for i in range(PLANES)]
        store(pl.multiple_of(at, SUB), functools.reduce(jnp.add, planes))

    def own(k, carry):
        store(pl.multiple_of(SUB + halo + k * SUB, SUB), cond[pl.ds(pl.multiple_of(k * SUB, SUB), SUB), :])
        return carry

    lax.fori_loop(0, rows // SUB, own, 0)

    def tile(k, carry):
        base = pl.multiple_of(k * SUB, SUB)
        plain = pl.ds(base, SUB)
        mid = [cond_pad[j, pl.ds(base + SUB, SUB), :] for j in range(width)]
        north, east, diagonal = [], [], []
        for j in range(width):
            up = cond_pad[j, pl.ds(base + SUB - 1, SUB), :]
            down = cond_pad[j, pl.ds(base + SUB + 1, SUB), :]
            if j + 1 < width:
                right = mid[j + 1]
            else:
                right = jnp.where(lanes == LANES - 1, 0.0, wrap_east(mid[0], lanes, width))
            left = mid[j - 1] if j else jnp.where(lanes == 0, 0.0, wrap_west(mid[-1], lanes, width))
            north.append(0.5 * (mid[j] + up))
            east.append(0.5 * (mid[j] + right))
            diagonal.append(north[j] + 0.5 * (mid[j] + down) + 0.5 * (mid[j] + left) + east[j])
        east[-1] = jnp.where(lanes == LANES - 1, 0.0, east[-1])
        for w in range(waves):
            q = []
            for j in range(width):
                full = diagonal[j] + squares[w] * mid[j]
                q.append(jnp.where(mid[j] > 0.0, lax.rsqrt(full), 0.0))
                root[w, j, plain, :] = full * q[j]
                inverse[w, j, plain, :] = q[j]
                q_pad[w, j, pl.ds(base + SUB, SUB), :] = q[j]
            for j in range(width):
                right = q[j + 1] if j + 1 < width else wrap_east(q[0], lanes, width)
                scaled = (2.0 / DELTA) * q[j]
                north_w = scaled * q_pad[w, j, pl.ds(base + SUB - 1, SUB), :] * north[j]
                east_w = scaled * right * east[j]
                for s in range(pair):
                    spot = pl.ds((base + 1) * SUB + w * pair + s, SUB, stride=SUB)
                    c_north[j, spot, :] = north_w
                    c_east[j, spot, :] = east_w
                    if j == 0:
                        q_first[spot, :] = jnp.where(lanes == 0, q[0], 0.0)
                    if j == width - 1:
                        c_wrap[spot, :] = jnp.where(lanes == 0, 0.0, wrap_west(east_w, lanes, width))
        return carry

    lax.fori_loop(0, tall // SUB, tile, 0)


def pack_kernel(order, fields, cond, near, across, near_rest, across_rest, edge, edge_sems, sems):
    waves, sources, rows, _ = fields.shape
    groups = len(order)
    pair = sources // groups
    halo = near.shape[1]
    wave_pos = lax.axis_index("wave")
    low = lax.rem(lax.axis_index("tile"), 2) == 0
    ends = jnp.where(low, rows - halo, 0), jnp.where(low, 0, rows - halo)
    edges = [
        pltpu.make_async_copy(
            cond.at[pl.ds(pl.multiple_of(end, halo), halo), :], edge.at[i], edge_sems.at[i]
        )
        for i, end in enumerate(ends)
    ]
    for copy in edges:
        copy.start()
    copies = []
    for k, shift in enumerate(order):
        chunk = lax.rem(wave_pos + shift, groups)
        for (first, rest), end in zip(((across, across_rest), (near, near_rest)), ends[::-1]):
            for w in range(waves):
                source = fields.at[
                    w, pl.ds(chunk * pair, pair), pl.ds(pl.multiple_of(end, halo), halo), :
                ]
                if k == 0:
                    target = first.at[pl.ds(w * pair, pair)]
                else:
                    target = rest.at[pl.ds((w * (groups - 1) + k - 1) * pair, pair)]
                copies.append(pltpu.make_async_copy(source, target, sems.at[len(copies)]))
    for copy in copies:
        copy.start()
    for k, ref in enumerate((near, across)):
        edges[k].wait()
        value = edge[k]
        for i in range(PLANES):
            part = value.astype(jnp.bfloat16)
            ref[SUB + i] = part
            value = value - part.astype(jnp.float32)
    for copy in copies:
        copy.wait()


def sweep_kernel(
    shift, place, counts, weights, cells, pairs,
    near, own, across, c_north, c_east, c_wrap, root, inverse, q_first,
    out, u_even, u_odd, inject,
):
    waves, sources, rows, cols = own.shape
    halo = near.shape[1]
    pair = out.shape[0]
    per, skip = place
    tall = rows + 2 * halo
    width = cols // LANES
    wave_pos = lax.axis_index("wave")
    first_row = lax.axis_index("tile") * rows
    first_wave = wave_pos * waves
    chunk = lax.rem(wave_pos + shift, sources // pair)
    count = [counts[first_wave + w] for w in range(waves)]
    limit = functools.reduce(jnp.maximum, count)
    least = functools.reduce(jnp.minimum, count)
    ids = lax.broadcasted_iota(jnp.int32, (SUB, LANES), 0)
    lanes = lax.broadcasted_iota(jnp.int32, (SUB, LANES), 1)
    count_of = functools.reduce(
        lambda v, w: jnp.where(lax.div(ids, pair) == w, count[w], v), range(waves), jnp.zeros_like(ids)
    )

    def spot_of(r):
        return pl.ds(pl.multiple_of(r * SUB, SUB), SUB)

    wide = lax.broadcasted_iota(jnp.int32, (2 * SUB, LANES), 1)

    def begin_tile(bases, load):
        for w in range(waves):
            for s in range(pair):
                for j, part in enumerate(exchange(pieces(load(w, s)), wide)):
                    part = part.astype(jnp.float32)
                    for half, base in enumerate(bases):
                        spot = pl.ds((base + 1) * SUB + w * pair + s, SUB, stride=SUB)
                        u_even[j, spot, :] = (
                            part[half * SUB:(half + 1) * SUB] * root[w, j, pl.ds(base, SUB), :]
                        )

    def begin_own(k, carry):
        at = pl.multiple_of(k * 2 * SUB, 2 * SUB)
        base = pl.multiple_of(halo + at, SUB)
        begin_tile((base, base + SUB), lambda w, s: own[w, chunk * pair + s, pl.ds(at, 2 * SUB), :])
        return carry

    lax.fori_loop(0, rows // (2 * SUB), begin_own, 0)
    low = lax.rem(lax.axis_index("tile"), 2) == 0
    begin_tile(
        (
            pl.multiple_of(jnp.where(low, halo + rows, 0), SUB),
            pl.multiple_of(jnp.where(low, 0, halo + rows), SUB),
        ),
        lambda w, s: jnp.concatenate([ref[w * per + skip + s] for ref in (near, across)], axis=0),
    )

    def wipe(k, carry):
        inject[spot_of(k), :] = jnp.zeros((SUB, LANES), jnp.float32)
        return carry

    lax.fori_loop(0, tall + 2, wipe, 0)
    for s in range(pair):
        for pole, sign in ((0, 1.0), (1, -1.0)):
            r = cells[pairs[chunk * pair + s, pole]] - first_row + halo

            @pl.when(jnp.logical_and(r >= 0, r < tall))
            def _():
                here = spot_of(r + 1)
                add = jnp.where(lax.rem(ids, pair) == s, q_first[here, :], 0.0)
                inject[here, :] = inject[here, :] + sign * add

    def level(t, src, dst, first):
        depth = limit - t + lax.rem(limit - t, 2)
        begin = halo - depth + 1
        boost = pick([0.0, CURRENT / DELTA] + [2.0 * CURRENT / DELTA * v for v in TABLE[1:ITERS]], t)
        live = count_of >= t

        def group(r, size, masked):
            spots = [spot_of(r + i - 1) for i in range(size + 2)]
            inner = range(1, size + 1)
            load = lambda ref, j, many: {i: ref[j, spots[i], :] for i in many}
            around = range(size + 2)
            start = load(src, 0, around)
            final = load(src, width - 1, around)
            past = {i: c_wrap[spots[i], :] * wrap_west(final[i], lanes, width) for i in inner}
            mid = start
            for j in range(width):
                if j + 1 < width - 1:
                    after = load(src, j + 1, around)
                elif j + 1 == width - 1:
                    after = final
                else:
                    after = {i: wrap_east(start[i], lanes, width) for i in inner}
                north = load(c_north, j, range(1, size + 2))
                east = load(c_east, j, inner)
                before = past
                past = {i: east[i] * mid[i] for i in inner}
                for i in inner:
                    total = (
                        (north[i] * mid[i - 1] + north[i + 1] * mid[i + 1])
                        + (east[i] * after[i] + before[i])
                    )
                    if first:
                        total = 0.5 * (total + DIAG * mid[i])
                    else:
                        total = total + (DIAG * mid[i] - dst[j, spots[i], :])
                    if j == 0:
                        total = total + boost * inject[spots[i], :]
                    if masked:
                        total = jnp.where(live, total, mid[i])
                    dst[j, spots[i], :] = total
                mid = after

        def loop(masked):
            def body(k, carry):
                group(begin + UNROLL * k, UNROLL, masked)
                return carry

            lax.fori_loop(0, (rows + 2 * depth) // UNROLL, body, 0)

        if first:
            loop(False)
        else:
            pl.when(t <= least)(lambda: loop(False))
            pl.when(t > least)(lambda: loop(True))

    level(1, u_even, u_odd, True)

    def two(k, carry):
        level(2 * k, u_odd, u_even, False)
        pl.when(2 * k + 1 <= limit)(lambda: level(2 * k + 1, u_even, u_odd, False))
        return carry

    lax.fori_loop(1, lax.div(limit, 2) + 1, two, 0)
    ends = [0.0] + [1.0 / v for v in TABLE[1:ITERS + 1]]
    gains = [weights[first_wave + w] * pick(ends, count[w]) for w in range(waves)]

    def finish(last):
        def body(k, carry):
            at = pl.multiple_of(k * SUB, SUB)
            base = at + halo
            for s in range(pair):
                sums = []
                for j in range(width):
                    terms = [
                        (gains[w] * inverse[w, j, pl.ds(base, SUB), :])
                        * last[j, pl.ds((base + 1) * SUB + w * pair + s, SUB, stride=SUB), :]
                        for w in range(waves)
                    ]
                    sums.append(functools.reduce(jnp.add, terms))
                for j, part in enumerate(exchange(sums, lanes)):
                    out[s, pl.ds(at, SUB), pl.ds(j * LANES, LANES)] = part
            return carry

        lax.fori_loop(0, rows // SUB, body, 0)

    pl.when(lax.rem(limit, 2) == 0)(lambda: finish(u_even))
    pl.when(lax.rem(limit, 2) == 1)(lambda: finish(u_odd))


def local(
    initial_fields, conductivity, wavenumbers, quad_weights, sweep_counts, electrode_cells,
    source_pairs,
):
    rows, cols = conductivity.shape
    waves, sources = initial_fields.shape[:2]
    halo = ITERS
    groups = lax.axis_size("wave")
    pair = sources // groups
    count = lax.axis_size("tile")
    order = [groups // 2] + [j for j in range(1, groups) if j != groups // 2] + [0]
    beside = [(i, i ^ 1) for i in range(count)]
    between = [(i, i + 1 if i % 2 else i - 1) for i in range(1, count - 1)]
    smem = pl.BlockSpec(memory_space=pltpu.SMEM)
    vmem = pl.BlockSpec(memory_space=pltpu.VMEM)
    bf16 = lambda *shape: jax.ShapeDtypeStruct(shape, jnp.bfloat16)
    ends = bf16(SUB + PLANES, halo, cols), bf16(SUB * (groups - 1), halo, cols)
    near, across, near_rest, across_rest = pl.pallas_call(
        functools.partial(pack_kernel, order),
        out_shape=(ends[0], ends[0], ends[1], ends[1]),
        in_specs=[pl.BlockSpec(memory_space=pltpu.HBM)] * 2,
        out_specs=[vmem] * 4,
        scratch_shapes=[
            pltpu.VMEM((2, halo, cols), jnp.float32),
            pltpu.SemaphoreType.DMA((2,)),
            pltpu.SemaphoreType.DMA((2 * waves * groups,)),
        ],
        compiler_params=pltpu.CompilerParams(vmem_limit_bytes=8 << 20),
        cost_estimate=pl.CostEstimate(flops=100000, bytes_accessed=2000000, transcendentals=0),
        name="pack",
    )(pltpu.with_memory_space_constraint(initial_fields, pltpu.HBM), pltpu.with_memory_space_constraint(conductivity, pltpu.HBM))
    across = lax.ppermute(across, "tile", between)
    near = lax.ppermute(near, "tile", beside)
    across_rest = lax.ppermute(across_rest, "tile", between)
    near_rest = lax.ppermute(near_rest, "tile", beside)
    tall = rows + 2 * halo
    width = cols // LANES
    high = (tall + 2) * SUB
    f32 = lambda *shape: jax.ShapeDtypeStruct(shape, jnp.float32)
    coefficients = pl.pallas_call(
        coefficients_kernel,
        out_shape=(
            f32(width, high, LANES), f32(width, high, LANES), f32(high, LANES),
            f32(waves, width, tall, LANES), f32(waves, width, tall, LANES), f32(high, LANES),
        ),
        in_specs=[smem, vmem, vmem, vmem],
        out_specs=[vmem] * 6,
        scratch_shapes=[
            pltpu.VMEM((width, tall + 2 * SUB, LANES), jnp.float32),
            pltpu.VMEM((waves, width, tall + SUB, LANES), jnp.float32),
        ],
        compiler_params=pltpu.CompilerParams(vmem_limit_bytes=16 << 20),
        cost_estimate=pl.CostEstimate(flops=4000000, bytes_accessed=6000000, transcendentals=0),
        name="coefficients",
    )(wavenumbers, near, conductivity, across)
    arrived = []
    for k, shift in enumerate(order):
        place = ((groups - 1) * pair, (k - 1) * pair) if k else (pair, 0)
        ends = (near_rest, across_rest) if k else (near, across)
        part = pl.pallas_call(
            functools.partial(sweep_kernel, shift, place),
            out_shape=f32(pair, rows, cols),
            in_specs=[smem] * 4 + [vmem] * 9,
            out_specs=vmem,
            scratch_shapes=[pltpu.VMEM((width, high, LANES), jnp.float32)] * 2
            + [pltpu.VMEM((high, LANES), jnp.float32)],
            compiler_params=pltpu.CompilerParams(vmem_limit_bytes=20 << 20),
            cost_estimate=pl.CostEstimate(flops=100000000, bytes_accessed=6000000, transcendentals=0),
        )(sweep_counts, quad_weights, electrode_cells, source_pairs, ends[0], initial_fields, ends[1], *coefficients)
        if shift:
            ring = [(i, (i + shift) % groups) for i in range(groups)]
            part = lax.ppermute(part, "wave", ring)
        arrived.append(part)
    return sum(arrived[1:], arrived[0])


def solution(mesh):
    placed = (P("wave", None, "tile", None), P("tile", None), P(), P(), P(), P(), P())
    return jax.shard_map(
        local, mesh=mesh, in_specs=placed, out_specs=P("wave", "tile", None), check_vma=False
    )
```

profile of v0, /device:TPU:19, one launch (start us, length us, event | category | flops | bytes accessed | tf_op | source)
XLA Modules:
  0.0 66.1 jit_solution(2706462476972094102)
XLA Ops:
  0.0 2.7 %pack.1 = (bf16[11,8,1024]{2,1,0:T(8,128)(2,1)}, bf16[11,8,1024]{2,1,0:T(8,128)(2,1)}, bf16[24,8,1024]{2,1,0:T(8,128)(2,1)}, bf16[24,8,1024]{2,1,0:T(8,128)(2,1)}) custom-call(bf16[4,8,32,1024]{3,2,1,0:T(8,128)(2,1)} %own.7, f32[32,1024]{1,0:T(8,128)} %cond.3), custom_call_target="tpu_custom_call" | custom-call | flops 100000 | bytes 2000000 | tf_op jit(solution)/shard_map/pack/pallas_call | solution.py:374
  2.8 0.7 %collective-permute-start.3 = (bf16[24,8,1024]{2,1,0:T(8,128)(2,1)}, bf16[24,8,1024]{2,1,0:T(8,128)(2,1)S(1)}, u32[]{:S(2)}, u32[]{:S(2)}) collective-permute-start(bf16[24,8,1024]{2,1,0:T(8,128)(2,1)} %get-tuple-element.23), channel_id=1, source_target_pairs={{0,1},{1,0},{2,3},{3,2},{4,5},{5,4},{6,7},{7,6},{8,9},{9,8},{10,11... | collective-permute-start | bytes 1179656 | tf_op jit(solution)/shard_map/ppermute | solution.py:391
  3.5 3.0 %collective-permute-start.4 = (bf16[24,8,1024]{2,1,0:T(8,128)(2,1)}, bf16[24,8,1024]{2,1,0:T(8,128)(2,1)S(1)}, u32[]{:S(2)}, u32[]{:S(2)}) collective-permute-start(bf16[24,8,1024]{2,1,0:T(8,128)(2,1)} %get-tuple-element.24), channel_id=1, source_target_pairs={{1,2},{2,1},{3,4},{4,3},{5,6},{6,5},{9,10},{10,9},{11,12},{12,11},... | collective-permute-start | bytes 1179656 | tf_op jit(solution)/shard_map/ppermute | solution.py:390
  6.5 0.1 collective-permute-start
  6.6 3.5 %collective-permute-start.1 = (bf16[11,8,1024]{2,1,0:T(8,128)(2,1)}, bf16[11,8,1024]{2,1,0:T(8,128)(2,1)S(1)}, u32[]{:S(2)}, u32[]{:S(2)}) collective-permute-start(bf16[11,8,1024]{2,1,0:T(8,128)(2,1)} %get-tuple-element.16), channel_id=1, source_target_pairs={{1,2},{2,1},{3,4},{4,3},{5,6},{6,5},{9,10},{10,9},{11,12},{12,11},... | collective-permute-start | bytes 540680 | tf_op jit(solution)/shard_map/ppermute | solution.py:388
  10.1 0.1 copy.8.pairs
  10.2 0.0 collective-permute-done.near
  10.2 11.0 %collective-permute-done.1.across = bf16[11,8,1024]{2,1,0:T(8,128)(2,1)S(1)} collective-permute-done((bf16[11,8,1024]{2,1,0:T(8,128)(2,1)}, bf16[11,8,1024]{2,1,0:T(8,128)(2,1)S(1)}, u32[]{:S(2)}, u32[]{:S(2)}) %collective-permute-start.1) | collective-permute-done | bytes 180256 | tf_op jit(solution)/shard_map/ppermute | solution.py:388
  21.2 0.0 copy-done.5
  21.2 3.1 %coefficients.1 = (f32[8,400,128]{2,1,0:T(8,128)S(1)}, f32[8,400,128]{2,1,0:T(8,128)S(1)}, f32[400,128]{1,0:T(8,128)S(1)}, f32[4,8,48,128]{3,2,1,0:T(8,128)S(1)}...) custom-call(f32[16]{0:T(128)S(1)} %copy-done.5, bf16[11,8,1024]{2,1,0:T(8,128)(2,1)S(1)} %collective-permute-done.near, ...), custom_call_target="tpu_custom_call" | custom-call | flops 4000000 | bytes 6000000 | tf_op jit(solution)/shard_map/coefficients/pallas_call | solution.py:396
  24.2 0.0 copy-done
  24.3 10.2 %shard_map.73 = f32[2,32,1024]{2,1,0:T(8,128)S(1)} custom-call(s32[16]{0:T(128)S(1)} %copy-done.2, f32[16]{0:T(128)S(1)} %copy-done.3, s32[64]{0:T(128)S(1)} %copy-done.4, s32[8,2]{1,0:T(8,128)S(1)} %copy.8.pairs, bf16[11,8,1024]{2,1,0:T(8,128)(2,1)S(1)} %collective-permute-done.near, bf16[4,8,32,1024]{3,2,1,0:T(8,128)(2,1)S(1)} %copy-done, ...), custom_call_target="tpu_custom_call" | custom-call | flops 100000000 | bytes 6000000 | tf_op jit(solution)/shard_map/pallas_call | solution.py:416
  34.5 0.1 collective-permute-start.2
  34.6 0.0 collective-permute-done.3.near
  34.6 0.0 collective-permute-done.4.across
  34.6 10.2 %shard_map.74 = f32[2,32,1024]{2,1,0:T(8,128)S(1)} custom-call(s32[16]{0:T(128)S(1)} %copy-done.2, f32[16]{0:T(128)S(1)} %copy-done.3, s32[64]{0:T(128)S(1)} %copy-done.4, s32[8,2]{1,0:T(8,128)S(1)} %copy.8.pairs, bf16[24,8,1024]{2,1,0:T(8,128)(2,1)S(1)} %collective-permute-done.3.near, bf16[4,8,32,1024]{3,2,1,0:T(8,128)(2,1)S(1)} %copy-done, ...), custom_call_target="tpu_custom_call" | custom-call | flops 100000000 | bytes 6000000 | tf_op jit(solution)/shard_map/pallas_call | solution.py:416
  44.8 0.1 collective-permute-start.5
  44.8 10.2 %shard_map.75 = f32[2,32,1024]{2,1,0:T(8,128)S(1)} custom-call(s32[16]{0:T(128)S(1)} %copy-done.2, f32[16]{0:T(128)S(1)} %copy-done.3, s32[64]{0:T(128)S(1)} %copy-done.4, s32[8,2]{1,0:T(8,128)S(1)} %copy.8.pairs, bf16[24,8,1024]{2,1,0:T(8,128)(2,1)S(1)} %collective-permute-done.3.near, bf16[4,8,32,1024]{3,2,1,0:T(8,128)(2,1)S(1)} %copy-done, ...), custom_call_target="tpu_custom_call" | custom-call | flops 100000000 | bytes 6000000 | tf_op jit(solution)/shard_map/pallas_call | solution.py:416
  55.1 0.1 collective-permute-start.6
  55.1 10.2 %shard_map.76 = f32[2,32,1024]{2,1,0:T(8,128)S(1)} custom-call(s32[16]{0:T(128)S(1)} %copy-done.2, f32[16]{0:T(128)S(1)} %copy-done.3, s32[64]{0:T(128)S(1)} %copy-done.4, s32[8,2]{1,0:T(8,128)S(1)} %copy.8.pairs, bf16[24,8,1024]{2,1,0:T(8,128)(2,1)S(1)} %collective-permute-done.3.near, bf16[4,8,32,1024]{3,2,1,0:T(8,128)(2,1)S(1)} %copy-done, ...), custom_call_target="tpu_custom_call" | custom-call | flops 100000000 | bytes 6000000 | tf_op jit(solution)/shard_map/pallas_call | solution.py:416
  65.3 0.0 collective-permute-done.2
  65.3 0.0 collective-permute-done.5
  65.3 0.0 collective-permute-done.6
  65.4 0.8 %add_add_fusion = f32[2,32,1024]{2,1,0:T(8,128)} fusion(f32[2,32,1024]{2,1,0:T(8,128)S(1)} %shard_map.76, f32[2,32,1024]{2,1,0:T(8,128)S(1)} %collective-permute-done.6, f32[2,32,1024]{2,1,0:T(8,128)S(1)} %collective-permute-done.2, f32[2,32,1024]{2,1,0:T(8,128)S(1)} %collective-permute-done.5), kind=kLoop, calls=%fused_computation | loop fusion | flops 196608 | bytes 1310720 | tf_op jit(solution)/shard_map/add | solution.py:430
  (12 shorter events, 0.0 us)
Async XLA Ops:
  0.0 24.2 %copy-start = (bf16[4,8,32,1024]{3,2,1,0:T(8,128)(2,1)S(1)}, bf16[4,8,32,1024]{3,2,1,0:T(8,128)(2,1)}, u32[]{:S(2)}) copy-start(bf16[4,8,32,1024]{3,2,1,0:T(8,128)(2,1)} %own.7) | copy-start | bytes 6291460
  0.0 21.2 %copy-start.1 = (f32[32,1024]{1,0:T(8,128)S(1)}, f32[32,1024]{1,0:T(8,128)}, u32[]{:S(2)}) copy-start(f32[32,1024]{1,0:T(8,128)} %cond.3) | copy-start | bytes 393220
  0.0 10.1 %copy-start.6 = (s32[8,2]{0,1:T(2,128)S(1)}, s32[8,2]{0,1:T(2,128)}, u32[]{:S(2)}) copy-start(s32[8,2]{0,1:T(2,128)} %param.13) | copy-start | bytes 196
  0.0 21.2 %copy-start.5 = (f32[16]{0:T(128)S(1)}, f32[16]{0:T(128)}, u32[]{:S(2)}) copy-start(f32[16]{0:T(128)} %wavenumbers.1) | copy-start | bytes 196
  0.0 24.2 %copy-start.4 = (s32[64]{0:T(128)S(1)}, s32[64]{0:T(128)}, u32[]{:S(2)}) copy-start(s32[64]{0:T(128)} %cells.7) | copy-start | bytes 772
  0.0 24.2 %copy-start.2 = (s32[16]{0:T(128)S(1)}, s32[16]{0:T(128)}, u32[]{:S(2)}) copy-start(s32[16]{0:T(128)} %counts.7) | copy-start | bytes 196
  0.0 24.2 %copy-start.3 = (f32[16]{0:T(128)S(1)}, f32[16]{0:T(128)}, u32[]{:S(2)}) copy-start(f32[16]{0:T(128)} %weights.7) | copy-start | bytes 196
  2.8 31.8 %collective-permute-start.3 = (bf16[24,8,1024]{2,1,0:T(8,128)(2,1)}, bf16[24,8,1024]{2,1,0:T(8,128)(2,1)S(1)}, u32[]{:S(2)}, u32[]{:S(2)}) collective-permute-start(bf16[24,8,1024]{2,1,0:T(8,128)(2,1)} %get-tuple-element.23), channel_id=1, source_target_pairs={{0,1},{1,0},{2,3},{3,2},{4,5},{5,4},{6,7},{7,6},{8,9},{9,8},{10,11... | collective-permute-start | bytes 1179656 | tf_op jit(solution)/shard_map/ppermute | solution.py:391
  3.5 31.1 %collective-permute-start.4 = (bf16[24,8,1024]{2,1,0:T(8,128)(2,1)}, bf16[24,8,1024]{2,1,0:T(8,128)(2,1)S(1)}, u32[]{:S(2)}, u32[]{:S(2)}) collective-permute-start(bf16[24,8,1024]{2,1,0:T(8,128)(2,1)} %get-tuple-element.24), channel_id=1, source_target_pairs={{1,2},{2,1},{3,4},{4,3},{5,6},{6,5},{9,10},{10,9},{11,12},{12,11},... | collective-permute-start | bytes 1179656 | tf_op jit(solution)/shard_map/ppermute | solution.py:390
  6.5 3.7 %collective-permute-start = (bf16[11,8,1024]{2,1,0:T(8,128)(2,1)}, bf16[11,8,1024]{2,1,0:T(8,128)(2,1)S(1)}, u32[]{:S(2)}, u32[]{:S(2)}) collective-permute-start(bf16[11,8,1024]{2,1,0:T(8,128)(2,1)} %get-tuple-element.15), channel_id=1, source_target_pairs={{0,1},{1,0},{2,3},{3,2},{4,5},{5,4},{6,7},{7,6},{8,9},{9,8},{10,11... | collective-permute-start | bytes 540680 | tf_op jit(solution)/shard_map/ppermute | solution.py:389
  6.6 14.6 %collective-permute-start.1 = (bf16[11,8,1024]{2,1,0:T(8,128)(2,1)}, bf16[11,8,1024]{2,1,0:T(8,128)(2,1)S(1)}, u32[]{:S(2)}, u32[]{:S(2)}) collective-permute-start(bf16[11,8,1024]{2,1,0:T(8,128)(2,1)} %get-tuple-element.16), channel_id=1, source_target_pairs={{1,2},{2,1},{3,4},{4,3},{5,6},{6,5},{9,10},{10,9},{11,12},{12,11},... | collective-permute-start | bytes 540680 | tf_op jit(solution)/shard_map/ppermute | solution.py:388
  34.5 30.8 %collective-permute-start.2 = (f32[2,32,1024]{2,1,0:T(8,128)S(1)}, f32[2,32,1024]{2,1,0:T(8,128)S(1)}, u32[]{:S(2)}, u32[]{:S(2)}) collective-permute-start(f32[2,32,1024]{2,1,0:T(8,128)S(1)} %shard_map.73), channel_id=1, source_target_pairs={{0,16},{8,24},{16,0},{24,8},{1,17},{9,25},{17,1},{25,9},{2,18},{10... | collective-permute-start | bytes 786440 | tf_op jit(solution)/shard_map/ppermute | solution.py:428
  44.8 20.6 %collective-permute-start.5 = (f32[2,32,1024]{2,1,0:T(8,128)S(1)}, f32[2,32,1024]{2,1,0:T(8,128)S(1)}, u32[]{:S(2)}, u32[]{:S(2)}) collective-permute-start(f32[2,32,1024]{2,1,0:T(8,128)S(1)} %shard_map.74), channel_id=1, source_target_pairs={{0,8},{8,16},{16,24},{24,0},{1,9},{9,17},{17,25},{25,1},{2,10},{10... | collective-permute-start | bytes 786440 | tf_op jit(solution)/shard_map/ppermute | solution.py:428
  55.1 10.3 %collective-permute-start.6 = (f32[2,32,1024]{2,1,0:T(8,128)S(1)}, f32[2,32,1024]{2,1,0:T(8,128)S(1)}, u32[]{:S(2)}, u32[]{:S(2)}) collective-permute-start(f32[2,32,1024]{2,1,0:T(8,128)S(1)} %shard_map.75), channel_id=1, source_target_pairs={{0,24},{8,0},{16,8},{24,16},{1,25},{9,1},{17,9},{25,17},{2,26},{10... | collective-permute-start | bytes 786440 | tf_op jit(solution)/shard_map/ppermute | solution.py:428
where the time goes:
time: 66.3 us; the launch traced here: 66.1 us
  Pallas kernels  46.6 us (70%)
  waiting for transfers between devices  11 us (17%)
  starting transfers between devices  7.51 us (11%)
  other arithmetic  0.78 us (1%)
    pallas_call x4, Pallas kernels, local(): pl.pallas_call(functools.partial(sweep_kernel, shift, place), out_shape=f...  40.8 us
    ppermute x1, waiting for transfers between devices, local(): across = lax.ppermute(across, 'tile', between)  11 us
    ppermute x1, starting transfers between devices, local(): across = lax.ppermute(across, 'tile', between)  3.49 us
    pallas_call x1, Pallas kernels, local(): pl.pallas_call(coefficients_kernel, out_shape=(f32(width, high, LANES), f...  3.07 us
    ppermute x1, starting transfers between devices, local(): across_rest = lax.ppermute(across_rest, 'tile', between)  3.02 us
    pallas_call x1, Pallas kernels, local(): pl.pallas_call(functools.partial(pack_kernel, order), out_shape=(ends[0],...  2.7 us
  transfers between devices with their start and end apart: 7, of which 1 were waited for; matrix products, arithmetic and copies ran while one was open for 0% of the time, Pallas kernels for 66%

commit v1 on v0

--- a/solution.py
+++ b/solution.py
@@ -19,6 +19,7 @@
 LANES = 128
 SUB = 8
 UNROLL = 4
+BATCH = 8
 PLANES = 3
 
 
@@ -266,27 +267,30 @@
                 inject[here, :] = inject[here, :] + sign * add
 
     def level(t, src, dst, first):
-        depth = limit - t + lax.rem(limit - t, 2)
+        depth = lax.div(limit - t + 3, 4) * 4
         begin = halo - depth + 1
         boost = pick([0.0, CURRENT / DELTA] + [2.0 * CURRENT / DELTA * v for v in TABLE[1:ITERS]], t)
         live = count_of >= t
 
-        def group(r, size, masked):
+        def wraps(r, size):
+            spots = [spot_of(r + i) for i in range(size)]
+            return (
+                [wrap_west(src[width - 1, spot, :], lanes, width) for spot in spots]
+                + [wrap_east(src[0, spot, :], lanes, width) for spot in spots]
+            )
+
+        def group(r, size, masked, turned):
             spots = [spot_of(r + i - 1) for i in range(size + 2)]
             inner = range(1, size + 1)
             load = lambda ref, j, many: {i: ref[j, spots[i], :] for i in many}
             around = range(size + 2)
-            start = load(src, 0, around)
-            final = load(src, width - 1, around)
-            past = {i: c_wrap[spots[i], :] * wrap_west(final[i], lanes, width) for i in inner}
-            mid = start
+            past = {i: c_wrap[spots[i], :] * turned[i - 1] for i in inner}
+            mid = load(src, 0, around)
             for j in range(width):
-                if j + 1 < width - 1:
+                if j + 1 < width:
                     after = load(src, j + 1, around)
-                elif j + 1 == width - 1:
-                    after = final
                 else:
-                    after = {i: wrap_east(start[i], lanes, width) for i in inner}
+                    after = {i: turned[size + i - 1] for i in inner}
                 north = load(c_north, j, range(1, size + 2))
                 east = load(c_east, j, inner)
                 before = past
@@ -309,10 +313,16 @@
 
         def loop(masked):
             def body(k, carry):
-                group(begin + UNROLL * k, UNROLL, masked)
+                r = begin + BATCH * k
+                turned = wraps(r, BATCH)
+                for i in range(0, BATCH, UNROLL):
+                    group(
+                        r + i, UNROLL, masked,
+                        turned[i:i + UNROLL] + turned[BATCH + i:BATCH + i + UNROLL],
+                    )
                 return carry
 
-            lax.fori_loop(0, (rows + 2 * depth) // UNROLL, body, 0)
+            lax.fori_loop(0, (rows + 2 * depth) // BATCH, body, 0)
 
         if first:
             loop(False)

time: 66.3 us -> 56.6 us (0.85)
  Pallas kernels: 46.6 us -> 36.9 us
    pallas_call x4, Pallas kernels: 40.8 us -> 31.1 us  [local(): pl.pallas_call(functools.partial(sweep_kernel, shift, place), out_shape=f...]
  transfers between devices with their start and end apart: 7 -> 7, of which waited for: 1 -> 1; matrix products, arithmetic and copies ran while one was open for 0% -> 0% of each run, Pallas kernels for 66% -> 61%
where the time goes in v1:
time: 56.6 us; the launch traced here: 56.5 us
  Pallas kernels  36.9 us (65%)
  waiting for transfers between devices  11 us (19%)
  starting transfers between devices  7.51 us (13%)
  other arithmetic  0.78 us (1%)
    pallas_call x4, Pallas kernels, local(): pl.pallas_call(functools.partial(sweep_kernel, shift, place), out_shape=f...  31.1 us
    ppermute x1, waiting for transfers between devices, local(): across = lax.ppermute(across, 'tile', between)  11 us
    ppermute x1, starting transfers between devices, local(): across = lax.ppermute(across, 'tile', between)  3.49 us
    pallas_call x1, Pallas kernels, local(): pl.pallas_call(coefficients_kernel, out_shape=(f32(width, high, LANES), f...  3.07 us
    ppermute x1, starting transfers between devices, local(): across_rest = lax.ppermute(across_rest, 'tile', between)  3.02 us
    pallas_call x1, Pallas kernels, local(): pl.pallas_call(functools.partial(pack_kernel, order), out_shape=(ends[0],...  2.7 us
  transfers between devices with their start and end apart: 7, of which 1 were waited for; matrix products, arithmetic and copies ran while one was open for 0% of the time, Pallas kernels for 61%

profile of v1, /device:TPU:19, one launch (start us, length us, event | category | flops | bytes accessed | tf_op | source)
XLA Modules:
  0.0 56.5 jit_solution(11887192296664026902)
XLA Ops:
  0.0 2.7 %pack.1 = (bf16[11,8,1024]{2,1,0:T(8,128)(2,1)}, bf16[11,8,1024]{2,1,0:T(8,128)(2,1)}, bf16[24,8,1024]{2,1,0:T(8,128)(2,1)}, bf16[24,8,1024]{2,1,0:T(8,128)(2,1)}) custom-call(bf16[4,8,32,1024]{3,2,1,0:T(8,128)(2,1)} %own.7, f32[32,1024]{1,0:T(8,128)} %cond.3), custom_call_target="tpu_custom_call" | custom-call | flops 100000 | bytes 2000000 | tf_op jit(solution)/shard_map/pack/pallas_call | solution.py:384
  2.8 0.7 %collective-permute-start.3 = (bf16[24,8,1024]{2,1,0:T(8,128)(2,1)}, bf16[24,8,1024]{2,1,0:T(8,128)(2,1)S(1)}, u32[]{:S(2)}, u32[]{:S(2)}) collective-permute-start(bf16[24,8,1024]{2,1,0:T(8,128)(2,1)} %get-tuple-element.23), channel_id=1, source_target_pairs={{0,1},{1,0},{2,3},{3,2},{4,5},{5,4},{6,7},{7,6},{8,9},{9,8},{10,11... | collective-permute-start | bytes 1179656 | tf_op jit(solution)/shard_map/ppermute | solution.py:401
  3.5 3.0 %collective-permute-start.4 = (bf16[24,8,1024]{2,1,0:T(8,128)(2,1)}, bf16[24,8,1024]{2,1,0:T(8,128)(2,1)S(1)}, u32[]{:S(2)}, u32[]{:S(2)}) collective-permute-start(bf16[24,8,1024]{2,1,0:T(8,128)(2,1)} %get-tuple-element.24), channel_id=1, source_target_pairs={{1,2},{2,1},{3,4},{4,3},{5,6},{6,5},{9,10},{10,9},{11,12},{12,11},... | collective-permute-start | bytes 1179656 | tf_op jit(solution)/shard_map/ppermute | solution.py:400
  6.5 0.1 collective-permute-start
  6.6 3.5 %collective-permute-start.1 = (bf16[11,8,1024]{2,1,0:T(8,128)(2,1)}, bf16[11,8,1024]{2,1,0:T(8,128)(2,1)S(1)}, u32[]{:S(2)}, u32[]{:S(2)}) collective-permute-start(bf16[11,8,1024]{2,1,0:T(8,128)(2,1)} %get-tuple-element.16), channel_id=1, source_target_pairs={{1,2},{2,1},{3,4},{4,3},{5,6},{6,5},{9,10},{10,9},{11,12},{12,11},... | collective-permute-start | bytes 540680 | tf_op jit(solution)/shard_map/ppermute | solution.py:398
  10.1 0.1 copy.8.pairs
  10.2 0.0 collective-permute-done.near
  10.2 11.0 %collective-permute-done.1.across = bf16[11,8,1024]{2,1,0:T(8,128)(2,1)S(1)} collective-permute-done((bf16[11,8,1024]{2,1,0:T(8,128)(2,1)}, bf16[11,8,1024]{2,1,0:T(8,128)(2,1)S(1)}, u32[]{:S(2)}, u32[]{:S(2)}) %collective-permute-start.1) | collective-permute-done | bytes 180256 | tf_op jit(solution)/shard_map/ppermute | solution.py:398
  21.2 0.0 copy-done.5
  21.2 3.1 %coefficients.1 = (f32[8,400,128]{2,1,0:T(8,128)S(1)}, f32[8,400,128]{2,1,0:T(8,128)S(1)}, f32[400,128]{1,0:T(8,128)S(1)}, f32[4,8,48,128]{3,2,1,0:T(8,128)S(1)}...) custom-call(f32[16]{0:T(128)S(1)} %copy-done.5, bf16[11,8,1024]{2,1,0:T(8,128)(2,1)S(1)} %collective-permute-done.near, ...), custom_call_target="tpu_custom_call" | custom-call | flops 4000000 | bytes 6000000 | tf_op jit(solution)/shard_map/coefficients/pallas_call | solution.py:406
  24.2 0.0 copy-done
  24.3 7.8 %shard_map.73 = f32[2,32,1024]{2,1,0:T(8,128)S(1)} custom-call(s32[16]{0:T(128)S(1)} %copy-done.2, f32[16]{0:T(128)S(1)} %copy-done.3, s32[64]{0:T(128)S(1)} %copy-done.4, s32[8,2]{1,0:T(8,128)S(1)} %copy.8.pairs, bf16[11,8,1024]{2,1,0:T(8,128)(2,1)S(1)} %collective-permute-done.near, bf16[4,8,32,1024]{3,2,1,0:T(8,128)(2,1)S(1)} %copy-done, ...), custom_call_target="tpu_custom_call" | custom-call | flops 100000000 | bytes 6000000 | tf_op jit(solution)/shard_map/pallas_call | solution.py:426
  32.1 0.1 collective-permute-start.2
  32.1 0.0 collective-permute-done.3.near
  32.2 0.0 collective-permute-done.4.across
  32.2 7.8 %shard_map.74 = f32[2,32,1024]{2,1,0:T(8,128)S(1)} custom-call(s32[16]{0:T(128)S(1)} %copy-done.2, f32[16]{0:T(128)S(1)} %copy-done.3, s32[64]{0:T(128)S(1)} %copy-done.4, s32[8,2]{1,0:T(8,128)S(1)} %copy.8.pairs, bf16[24,8,1024]{2,1,0:T(8,128)(2,1)S(1)} %collective-permute-done.3.near, bf16[4,8,32,1024]{3,2,1,0:T(8,128)(2,1)S(1)} %copy-done, ...), custom_call_target="tpu_custom_call" | custom-call | flops 100000000 | bytes 6000000 | tf_op jit(solution)/shard_map/pallas_call | solution.py:426
  40.0 0.1 collective-permute-start.5
  40.0 7.8 %shard_map.75 = f32[2,32,1024]{2,1,0:T(8,128)S(1)} custom-call(s32[16]{0:T(128)S(1)} %copy-done.2, f32[16]{0:T(128)S(1)} %copy-done.3, s32[64]{0:T(128)S(1)} %copy-done.4, s32[8,2]{1,0:T(8,128)S(1)} %copy.8.pairs, bf16[24,8,1024]{2,1,0:T(8,128)(2,1)S(1)} %collective-permute-done.3.near, bf16[4,8,32,1024]{3,2,1,0:T(8,128)(2,1)S(1)} %copy-done, ...), custom_call_target="tpu_custom_call" | custom-call | flops 100000000 | bytes 6000000 | tf_op jit(solution)/shard_map/pallas_call | solution.py:426
  47.8 0.1 collective-permute-start.6
  47.9 7.8 %shard_map.76 = f32[2,32,1024]{2,1,0:T(8,128)S(1)} custom-call(s32[16]{0:T(128)S(1)} %copy-done.2, f32[16]{0:T(128)S(1)} %copy-done.3, s32[64]{0:T(128)S(1)} %copy-done.4, s32[8,2]{1,0:T(8,128)S(1)} %copy.8.pairs, bf16[24,8,1024]{2,1,0:T(8,128)(2,1)S(1)} %collective-permute-done.3.near, bf16[4,8,32,1024]{3,2,1,0:T(8,128)(2,1)S(1)} %copy-done, ...), custom_call_target="tpu_custom_call" | custom-call | flops 100000000 | bytes 6000000 | tf_op jit(solution)/shard_map/pallas_call | solution.py:426
  55.7 0.0 collective-permute-done.2
  55.7 0.0 collective-permute-done.5
  55.7 0.0 collective-permute-done.6
  55.7 0.8 %add_add_fusion = f32[2,32,1024]{2,1,0:T(8,128)} fusion(f32[2,32,1024]{2,1,0:T(8,128)S(1)} %shard_map.76, f32[2,32,1024]{2,1,0:T(8,128)S(1)} %collective-permute-done.6, f32[2,32,1024]{2,1,0:T(8,128)S(1)} %collective-permute-done.2, f32[2,32,1024]{2,1,0:T(8,128)S(1)} %collective-permute-done.5), kind=kLoop, calls=%fused_computation | loop fusion | flops 196608 | bytes 1310720 | tf_op jit(solution)/shard_map/add | solution.py:440
  (12 shorter events, 0.0 us)
Async XLA Ops:
  0.0 24.2 %copy-start = (bf16[4,8,32,1024]{3,2,1,0:T(8,128)(2,1)S(1)}, bf16[4,8,32,1024]{3,2,1,0:T(8,128)(2,1)}, u32[]{:S(2)}) copy-start(bf16[4,8,32,1024]{3,2,1,0:T(8,128)(2,1)} %own.7) | copy-start | bytes 6291460
  0.0 21.2 %copy-start.1 = (f32[32,1024]{1,0:T(8,128)S(1)}, f32[32,1024]{1,0:T(8,128)}, u32[]{:S(2)}) copy-start(f32[32,1024]{1,0:T(8,128)} %cond.3) | copy-start | bytes 393220
  0.0 10.1 %copy-start.6 = (s32[8,2]{0,1:T(2,128)S(1)}, s32[8,2]{0,1:T(2,128)}, u32[]{:S(2)}) copy-start(s32[8,2]{0,1:T(2,128)} %param.13) | copy-start | bytes 196
  0.0 21.2 %copy-start.5 = (f32[16]{0:T(128)S(1)}, f32[16]{0:T(128)}, u32[]{:S(2)}) copy-start(f32[16]{0:T(128)} %wavenumbers.1) | copy-start | bytes 196
  0.0 24.2 %copy-start.4 = (s32[64]{0:T(128)S(1)}, s32[64]{0:T(128)}, u32[]{:S(2)}) copy-start(s32[64]{0:T(128)} %cells.7) | copy-start | bytes 772
  0.0 24.2 %copy-start.2 = (s32[16]{0:T(128)S(1)}, s32[16]{0:T(128)}, u32[]{:S(2)}) copy-start(s32[16]{0:T(128)} %counts.7) | copy-start | bytes 196
  0.0 24.2 %copy-start.3 = (f32[16]{0:T(128)S(1)}, f32[16]{0:T(128)}, u32[]{:S(2)}) copy-start(f32[16]{0:T(128)} %weights.7) | copy-start | bytes 196
  2.8 29.4 %collective-permute-start.3 = (bf16[24,8,1024]{2,1,0:T(8,128)(2,1)}, bf16[24,8,1024]{2,1,0:T(8,128)(2,1)S(1)}, u32[]{:S(2)}, u32[]{:S(2)}) collective-permute-start(bf16[24,8,1024]{2,1,0:T(8,128)(2,1)} %get-tuple-element.23), channel_id=1, source_target_pairs={{0,1},{1,0},{2,3},{3,2},{4,5},{5,4},{6,7},{7,6},{8,9},{9,8},{10,11... | collective-permute-start | bytes 1179656 | tf_op jit(solution)/shard_map/ppermute | solution.py:401
  3.5 28.7 %collective-permute-start.4 = (bf16[24,8,1024]{2,1,0:T(8,128)(2,1)}, bf16[24,8,1024]{2,1,0:T(8,128)(2,1)S(1)}, u32[]{:S(2)}, u32[]{:S(2)}) collective-permute-start(bf16[24,8,1024]{2,1,0:T(8,128)(2,1)} %get-tuple-element.24), channel_id=1, source_target_pairs={{1,2},{2,1},{3,4},{4,3},{5,6},{6,5},{9,10},{10,9},{11,12},{12,11},... | collective-permute-start | bytes 1179656 | tf_op jit(solution)/shard_map/ppermute | solution.py:400
  6.5 3.7 %collective-permute-start = (bf16[11,8,1024]{2,1,0:T(8,128)(2,1)}, bf16[11,8,1024]{2,1,0:T(8,128)(2,1)S(1)}, u32[]{:S(2)}, u32[]{:S(2)}) collective-permute-start(bf16[11,8,1024]{2,1,0:T(8,128)(2,1)} %get-tuple-element.15), channel_id=1, source_target_pairs={{0,1},{1,0},{2,3},{3,2},{4,5},{5,4},{6,7},{7,6},{8,9},{9,8},{10,11... | collective-permute-start | bytes 540680 | tf_op jit(solution)/shard_map/ppermute | solution.py:399
  6.6 14.6 %collective-permute-start.1 = (bf16[11,8,1024]{2,1,0:T(8,128)(2,1)}, bf16[11,8,1024]{2,1,0:T(8,128)(2,1)S(1)}, u32[]{:S(2)}, u32[]{:S(2)}) collective-permute-start(bf16[11,8,1024]{2,1,0:T(8,128)(2,1)} %get-tuple-element.16), channel_id=1, source_target_pairs={{1,2},{2,1},{3,4},{4,3},{5,6},{6,5},{9,10},{10,9},{11,12},{12,11},... | collective-permute-start | bytes 540680 | tf_op jit(solution)/shard_map/ppermute | solution.py:398
  32.1 23.6 %collective-permute-start.2 = (f32[2,32,1024]{2,1,0:T(8,128)S(1)}, f32[2,32,1024]{2,1,0:T(8,128)S(1)}, u32[]{:S(2)}, u32[]{:S(2)}) collective-permute-start(f32[2,32,1024]{2,1,0:T(8,128)S(1)} %shard_map.73), channel_id=1, source_target_pairs={{0,16},{8,24},{16,0},{24,8},{1,17},{9,25},{17,1},{25,9},{2,18},{10... | collective-permute-start | bytes 786440 | tf_op jit(solution)/shard_map/ppermute | solution.py:438
  40.0 15.7 %collective-permute-start.5 = (f32[2,32,1024]{2,1,0:T(8,128)S(1)}, f32[2,32,1024]{2,1,0:T(8,128)S(1)}, u32[]{:S(2)}, u32[]{:S(2)}) collective-permute-start(f32[2,32,1024]{2,1,0:T(8,128)S(1)} %shard_map.74), channel_id=1, source_target_pairs={{0,8},{8,16},{16,24},{24,0},{1,9},{9,17},{17,25},{25,1},{2,10},{10... | collective-permute-start | bytes 786440 | tf_op jit(solution)/shard_map/ppermute | solution.py:438
  47.8 7.9 %collective-permute-start.6 = (f32[2,32,1024]{2,1,0:T(8,128)S(1)}, f32[2,32,1024]{2,1,0:T(8,128)S(1)}, u32[]{:S(2)}, u32[]{:S(2)}) collective-permute-start(f32[2,32,1024]{2,1,0:T(8,128)S(1)} %shard_map.75), channel_id=1, source_target_pairs={{0,24},{8,0},{16,8},{24,16},{1,25},{9,1},{17,9},{25,17},{2,26},{10... | collective-permute-start | bytes 786440 | tf_op jit(solution)/shard_map/ppermute | solution.py:438

commit v2 on v1

--- a/solution.py
+++ b/solution.py
@@ -104,11 +104,8 @@
         planes = [ref[SUB + i].astype(jnp.float32) for i in range(PLANES)]
         store(pl.multiple_of(at, SUB), functools.reduce(jnp.add, planes))
 
-    def own(k, carry):
-        store(pl.multiple_of(SUB + halo + k * SUB, SUB), cond[pl.ds(pl.multiple_of(k * SUB, SUB), SUB), :])
-        return carry
-
-    lax.fori_loop(0, rows // SUB, own, 0)
+    for k in range(rows // SUB):
+        store(SUB + halo + k * SUB, cond[pl.ds(k * SUB, SUB), :])
 
     def tile(k, carry):
         base = pl.multiple_of(k * SUB, SUB)
@@ -251,11 +248,7 @@
         lambda w, s: jnp.concatenate([ref[w * per + skip + s] for ref in (near, across)], axis=0),
     )
 
-    def wipe(k, carry):
-        inject[spot_of(k), :] = jnp.zeros((SUB, LANES), jnp.float32)
-        return carry
-
-    lax.fori_loop(0, tall + 2, wipe, 0)
+    inject[...] = jnp.zeros(inject.shape, jnp.float32)
     for s in range(pair):
         for pole, sign in ((0, 1.0), (1, -1.0)):
             r = cells[pairs[chunk * pair + s, pole]] - first_row + halo
@@ -354,7 +347,7 @@
                         for w in range(waves)
                     ]
                     sums.append(functools.reduce(jnp.add, terms))
-                for j, part in enumerate(exchange(sums, lanes)):
+                for j, part in enumerate(sums):
                     out[s, pl.ds(at, SUB), pl.ds(j * LANES, LANES)] = part
             return carry
 
@@ -362,6 +355,11 @@
 
     pl.when(lax.rem(limit, 2) == 0)(lambda: finish(u_even))
     pl.when(lax.rem(limit, 2) == 1)(lambda: finish(u_odd))
+    for s in range(pair):
+        for k in range(rows // SUB):
+            cuts = [(s, pl.ds(k * SUB, SUB), pl.ds(j * LANES, LANES)) for j in range(width)]
+            for cut, part in zip(cuts, exchange([out[cut] for cut in cuts], lanes)):
+                out[cut] = part
 
 
 def local(

time: 56.6 us -> 54.3 us (0.959)
  the two profiles are of different devices: /device:TPU:19 before, /device:TPU:3 now
where the time goes in v2:
time: 54.3 us; the launch traced here: 54.1 us
  Pallas kernels  20.9 us (38%)
  starting transfers between devices  16.2 us (30%)
  waiting for transfers between devices  15.9 us (29%)
  other arithmetic  0.78 us (1%)
    pallas_call x4, Pallas kernels, local(): pl.pallas_call(functools.partial(sweep_kernel, shift, place), out_shape=f...  15.9 us
    ppermute x1, waiting for transfers between devices, local(): across = lax.ppermute(across, 'tile', between)  11 us
    ppermute x3, starting transfers between devices, local(): part = lax.ppermute(part, 'wave', ring)  8.86 us
    ppermute x3, waiting for transfers between devices, local(): part = lax.ppermute(part, 'wave', ring)  4.97 us
    ppermute x1, starting transfers between devices, local(): across = lax.ppermute(across, 'tile', between)  3.49 us
    ppermute x1, starting transfers between devices, local(): across_rest = lax.ppermute(across_rest, 'tile', between)  3.02 us
    pallas_call x1, Pallas kernels, local(): pl.pallas_call(functools.partial(pack_kernel, order), out_shape=(ends[0],...  2.7 us
    pallas_call x1, Pallas kernels, local(): pl.pallas_call(coefficients_kernel, out_shape=(f32(width, high, LANES), f...  2.27 us
  transfers between devices with their start and end apart: 7, of which 2 were waited for; matrix products, arithmetic and copies ran while one was open for 0% of the time, Pallas kernels for 34%

profile of v2, /device:TPU:3, one launch (start us, length us, event | category | flops | bytes accessed | tf_op | source)
XLA Modules:
  0.0 54.1 jit_solution(5684829190172423174)
XLA Ops:
  0.0 0.0 copy-start.5
  0.0 2.7 %pack.1 = (bf16[11,8,1024]{2,1,0:T(8,128)(2,1)}, bf16[11,8,1024]{2,1,0:T(8,128)(2,1)}, bf16[24,8,1024]{2,1,0:T(8,128)(2,1)}, bf16[24,8,1024]{2,1,0:T(8,128)(2,1)}) custom-call(bf16[4,8,32,1024]{3,2,1,0:T(8,128)(2,1)} %own.7, f32[32,1024]{1,0:T(8,128)} %cond.3), custom_call_target="tpu_custom_call" | custom-call | flops 100000 | bytes 2000000 | tf_op jit(solution)/shard_map/pack/pallas_call | solution.py:382
  2.8 0.7 %collective-permute-start.3 = (bf16[24,8,1024]{2,1,0:T(8,128)(2,1)}, bf16[24,8,1024]{2,1,0:T(8,128)(2,1)S(1)}, u32[]{:S(2)}, u32[]{:S(2)}) collective-permute-start(bf16[24,8,1024]{2,1,0:T(8,128)(2,1)} %get-tuple-element.23), channel_id=1, source_target_pairs={{0,1},{1,0},{2,3},{3,2},{4,5},{5,4},{6,7},{7,6},{8,9},{9,8},{10,11... | collective-permute-start | bytes 1179656 | tf_op jit(solution)/shard_map/ppermute | solution.py:399
  3.5 3.0 %collective-permute-start.4 = (bf16[24,8,1024]{2,1,0:T(8,128)(2,1)}, bf16[24,8,1024]{2,1,0:T(8,128)(2,1)S(1)}, u32[]{:S(2)}, u32[]{:S(2)}) collective-permute-start(bf16[24,8,1024]{2,1,0:T(8,128)(2,1)} %get-tuple-element.24), channel_id=1, source_target_pairs={{1,2},{2,1},{3,4},{4,3},{5,6},{6,5},{9,10},{10,9},{11,12},{12,11},... | collective-permute-start | bytes 1179656 | tf_op jit(solution)/shard_map/ppermute | solution.py:398
  6.5 0.1 collective-permute-start
  6.6 3.5 %collective-permute-start.1 = (bf16[11,8,1024]{2,1,0:T(8,128)(2,1)}, bf16[11,8,1024]{2,1,0:T(8,128)(2,1)S(1)}, u32[]{:S(2)}, u32[]{:S(2)}) collective-permute-start(bf16[11,8,1024]{2,1,0:T(8,128)(2,1)} %get-tuple-element.16), channel_id=1, source_target_pairs={{1,2},{2,1},{3,4},{4,3},{5,6},{6,5},{9,10},{10,9},{11,12},{12,11},... | collective-permute-start | bytes 540680 | tf_op jit(solution)/shard_map/ppermute | solution.py:396
  10.1 0.1 copy.8.pairs
  10.2 0.0 collective-permute-done.near
  10.2 11.0 %collective-permute-done.1.across = bf16[11,8,1024]{2,1,0:T(8,128)(2,1)S(1)} collective-permute-done((bf16[11,8,1024]{2,1,0:T(8,128)(2,1)}, bf16[11,8,1024]{2,1,0:T(8,128)(2,1)S(1)}, u32[]{:S(2)}, u32[]{:S(2)}) %collective-permute-start.1) | collective-permute-done | bytes 180256 | tf_op jit(solution)/shard_map/ppermute | solution.py:396
  21.2 2.3 %coefficients.1 = (f32[8,400,128]{2,1,0:T(8,128)S(1)}, f32[8,400,128]{2,1,0:T(8,128)S(1)}, f32[400,128]{1,0:T(8,128)S(1)}, f32[4,8,48,128]{3,2,1,0:T(8,128)S(1)}...) custom-call(f32[16]{0:T(128)S(1)} %copy-done.5, bf16[11,8,1024]{2,1,0:T(8,128)(2,1)S(1)} %collective-permute-done.near, ...), custom_call_target="tpu_custom_call" | custom-call | flops 4000000 | bytes 6000000 | tf_op jit(solution)/shard_map/coefficients/pallas_call | solution.py:404
  23.4 0.0 copy-done
  23.5 4.0 %shard_map.73 = f32[2,32,1024]{2,1,0:T(8,128)S(1)} custom-call(s32[16]{0:T(128)S(1)} %copy-done.2, f32[16]{0:T(128)S(1)} %copy-done.3, s32[64]{0:T(128)S(1)} %copy-done.4, s32[8,2]{1,0:T(8,128)S(1)} %copy.8.pairs, bf16[11,8,1024]{2,1,0:T(8,128)(2,1)S(1)} %collective-permute-done.near, bf16[4,8,32,1024]{3,2,1,0:T(8,128)(2,1)S(1)} %copy-done, ...), custom_call_target="tpu_custom_call" | custom-call | flops 100000000 | bytes 6000000 | tf_op jit(solution)/shard_map/pallas_call | solution.py:424
  27.5 5.4 %collective-permute-start.2 = (f32[2,32,1024]{2,1,0:T(8,128)S(1)}, f32[2,32,1024]{2,1,0:T(8,128)S(1)}, u32[]{:S(2)}, u32[]{:S(2)}) collective-permute-start(f32[2,32,1024]{2,1,0:T(8,128)S(1)} %shard_map.73), channel_id=1, source_target_pairs={{0,16},{8,24},{16,0},{24,8},{1,17},{9,25},{17,1},{25,9},{2,18},{10... | collective-permute-start | bytes 786440 | tf_op jit(solution)/shard_map/ppermute | solution.py:436
  32.9 0.0 collective-permute-done.3.near
  32.9 0.0 collective-permute-done.4.across
  32.9 4.0 %shard_map.74 = f32[2,32,1024]{2,1,0:T(8,128)S(1)} custom-call(s32[16]{0:T(128)S(1)} %copy-done.2, f32[16]{0:T(128)S(1)} %copy-done.3, s32[64]{0:T(128)S(1)} %copy-done.4, s32[8,2]{1,0:T(8,128)S(1)} %copy.8.pairs, bf16[24,8,1024]{2,1,0:T(8,128)(2,1)S(1)} %collective-permute-done.3.near, bf16[4,8,32,1024]{3,2,1,0:T(8,128)(2,1)S(1)} %copy-done, ...), custom_call_target="tpu_custom_call" | custom-call | flops 100000000 | bytes 6000000 | tf_op jit(solution)/shard_map/pallas_call | solution.py:424
  36.9 0.1 collective-permute-start.5
  37.0 4.0 %shard_map.75 = f32[2,32,1024]{2,1,0:T(8,128)S(1)} custom-call(s32[16]{0:T(128)S(1)} %copy-done.2, f32[16]{0:T(128)S(1)} %copy-done.3, s32[64]{0:T(128)S(1)} %copy-done.4, s32[8,2]{1,0:T(8,128)S(1)} %copy.8.pairs, bf16[24,8,1024]{2,1,0:T(8,128)(2,1)S(1)} %collective-permute-done.3.near, bf16[4,8,32,1024]{3,2,1,0:T(8,128)(2,1)S(1)} %copy-done, ...), custom_call_target="tpu_custom_call" | custom-call | flops 100000000 | bytes 6000000 | tf_op jit(solution)/shard_map/pallas_call | solution.py:424
  41.0 3.4 %collective-permute-start.6 = (f32[2,32,1024]{2,1,0:T(8,128)S(1)}, f32[2,32,1024]{2,1,0:T(8,128)S(1)}, u32[]{:S(2)}, u32[]{:S(2)}) collective-permute-start(f32[2,32,1024]{2,1,0:T(8,128)S(1)} %shard_map.75), channel_id=1, source_target_pairs={{0,24},{8,0},{16,8},{24,16},{1,25},{9,1},{17,9},{25,17},{2,26},{10... | collective-permute-start | bytes 786440 | tf_op jit(solution)/shard_map/ppermute | solution.py:436
  44.3 4.0 %shard_map.76 = f32[2,32,1024]{2,1,0:T(8,128)S(1)} custom-call(s32[16]{0:T(128)S(1)} %copy-done.2, f32[16]{0:T(128)S(1)} %copy-done.3, s32[64]{0:T(128)S(1)} %copy-done.4, s32[8,2]{1,0:T(8,128)S(1)} %copy.8.pairs, bf16[24,8,1024]{2,1,0:T(8,128)(2,1)S(1)} %collective-permute-done.3.near, bf16[4,8,32,1024]{3,2,1,0:T(8,128)(2,1)S(1)} %copy-done, ...), custom_call_target="tpu_custom_call" | custom-call | flops 100000000 | bytes 6000000 | tf_op jit(solution)/shard_map/pallas_call | solution.py:424
  48.3 0.0 collective-permute-done.2
  48.3 0.0 collective-permute-done.5
  48.3 5.0 %collective-permute-done.6 = f32[2,32,1024]{2,1,0:T(8,128)S(1)} collective-permute-done((f32[2,32,1024]{2,1,0:T(8,128)S(1)}, f32[2,32,1024]{2,1,0:T(8,128)S(1)}, u32[]{:S(2)}, u32[]{:S(2)}) %collective-permute-start.6) | collective-permute-done | bytes 262176 | tf_op jit(solution)/shard_map/ppermute | solution.py:436
  53.3 0.8 %add_add_fusion = f32[2,32,1024]{2,1,0:T(8,128)} fusion(f32[2,32,1024]{2,1,0:T(8,128)S(1)} %shard_map.76, f32[2,32,1024]{2,1,0:T(8,128)S(1)} %collective-permute-done.6, f32[2,32,1024]{2,1,0:T(8,128)S(1)} %collective-permute-done.2, f32[2,32,1024]{2,1,0:T(8,128)S(1)} %collective-permute-done.5), kind=kLoop, calls=%fused_computation | loop fusion | flops 196608 | bytes 1310720 | tf_op jit(solution)/shard_map/add | solution.py:438
  (12 shorter events, 0.0 us)
Async XLA Ops:
  0.0 23.4 %copy-start = (bf16[4,8,32,1024]{3,2,1,0:T(8,128)(2,1)S(1)}, bf16[4,8,32,1024]{3,2,1,0:T(8,128)(2,1)}, u32[]{:S(2)}) copy-start(bf16[4,8,32,1024]{3,2,1,0:T(8,128)(2,1)} %own.7) | copy-start | bytes 6291460
  0.0 21.2 %copy-start.1 = (f32[32,1024]{1,0:T(8,128)S(1)}, f32[32,1024]{1,0:T(8,128)}, u32[]{:S(2)}) copy-start(f32[32,1024]{1,0:T(8,128)} %cond.3) | copy-start | bytes 393220
  0.0 10.1 %copy-start.6 = (s32[8,2]{0,1:T(2,128)S(1)}, s32[8,2]{0,1:T(2,128)}, u32[]{:S(2)}) copy-start(s32[8,2]{0,1:T(2,128)} %param.13) | copy-start | bytes 196
  0.0 21.2 %copy-start.5 = (f32[16]{0:T(128)S(1)}, f32[16]{0:T(128)}, u32[]{:S(2)}) copy-start(f32[16]{0:T(128)} %wavenumbers.1) | copy-start | bytes 196
  0.0 23.4 %copy-start.4 = (s32[64]{0:T(128)S(1)}, s32[64]{0:T(128)}, u32[]{:S(2)}) copy-start(s32[64]{0:T(128)} %cells.7) | copy-start | bytes 772
  0.0 23.4 %copy-start.2 = (s32[16]{0:T(128)S(1)}, s32[16]{0:T(128)}, u32[]{:S(2)}) copy-start(s32[16]{0:T(128)} %counts.7) | copy-start | bytes 196
  0.0 23.4 %copy-start.3 = (f32[16]{0:T(128)S(1)}, f32[16]{0:T(128)}, u32[]{:S(2)}) copy-start(f32[16]{0:T(128)} %weights.7) | copy-start | bytes 196
  2.8 30.1 %collective-permute-start.3 = (bf16[24,8,1024]{2,1,0:T(8,128)(2,1)}, bf16[24,8,1024]{2,1,0:T(8,128)(2,1)S(1)}, u32[]{:S(2)}, u32[]{:S(2)}) collective-permute-start(bf16[24,8,1024]{2,1,0:T(8,128)(2,1)} %get-tuple-element.23), channel_id=1, source_target_pairs={{0,1},{1,0},{2,3},{3,2},{4,5},{5,4},{6,7},{7,6},{8,9},{9,8},{10,11... | collective-permute-start | bytes 1179656 | tf_op jit(solution)/shard_map/ppermute | solution.py:399
  3.5 29.4 %collective-permute-start.4 = (bf16[24,8,1024]{2,1,0:T(8,128)(2,1)}, bf16[24,8,1024]{2,1,0:T(8,128)(2,1)S(1)}, u32[]{:S(2)}, u32[]{:S(2)}) collective-permute-start(bf16[24,8,1024]{2,1,0:T(8,128)(2,1)} %get-tuple-element.24), channel_id=1, source_target_pairs={{1,2},{2,1},{3,4},{4,3},{5,6},{6,5},{9,10},{10,9},{11,12},{12,11},... | collective-permute-start | bytes 1179656 | tf_op jit(solution)/shard_map/ppermute | solution.py:398
  6.5 3.7 %collective-permute-start = (bf16[11,8,1024]{2,1,0:T(8,128)(2,1)}, bf16[11,8,1024]{2,1,0:T(8,128)(2,1)S(1)}, u32[]{:S(2)}, u32[]{:S(2)}) collective-permute-start(bf16[11,8,1024]{2,1,0:T(8,128)(2,1)} %get-tuple-element.15), channel_id=1, source_target_pairs={{0,1},{1,0},{2,3},{3,2},{4,5},{5,4},{6,7},{7,6},{8,9},{9,8},{10,11... | collective-permute-start | bytes 540680 | tf_op jit(solution)/shard_map/ppermute | solution.py:397
  6.6 14.6 %collective-permute-start.1 = (bf16[11,8,1024]{2,1,0:T(8,128)(2,1)}, bf16[11,8,1024]{2,1,0:T(8,128)(2,1)S(1)}, u32[]{:S(2)}, u32[]{:S(2)}) collective-permute-start(bf16[11,8,1024]{2,1,0:T(8,128)(2,1)} %get-tuple-element.16), channel_id=1, source_target_pairs={{1,2},{2,1},{3,4},{4,3},{5,6},{6,5},{9,10},{10,9},{11,12},{12,11},... | collective-permute-start | bytes 540680 | tf_op jit(solution)/shard_map/ppermute | solution.py:396
  27.5 20.9 %collective-permute-start.2 = (f32[2,32,1024]{2,1,0:T(8,128)S(1)}, f32[2,32,1024]{2,1,0:T(8,128)S(1)}, u32[]{:S(2)}, u32[]{:S(2)}) collective-permute-start(f32[2,32,1024]{2,1,0:T(8,128)S(1)} %shard_map.73), channel_id=1, source_target_pairs={{0,16},{8,24},{16,0},{24,8},{1,17},{9,25},{17,1},{25,9},{2,18},{10... | collective-permute-start | bytes 786440 | tf_op jit(solution)/shard_map/ppermute | solution.py:436
  36.9 11.4 %collective-permute-start.5 = (f32[2,32,1024]{2,1,0:T(8,128)S(1)}, f32[2,32,1024]{2,1,0:T(8,128)S(1)}, u32[]{:S(2)}, u32[]{:S(2)}) collective-permute-start(f32[2,32,1024]{2,1,0:T(8,128)S(1)} %shard_map.74), channel_id=1, source_target_pairs={{0,8},{8,16},{16,24},{24,0},{1,9},{9,17},{17,25},{25,1},{2,10},{10... | collective-permute-start | bytes 786440 | tf_op jit(solution)/shard_map/ppermute | solution.py:436
  41.0 12.3 %collective-permute-start.6 = (f32[2,32,1024]{2,1,0:T(8,128)S(1)}, f32[2,32,1024]{2,1,0:T(8,128)S(1)}, u32[]{:S(2)}, u32[]{:S(2)}) collective-permute-start(f32[2,32,1024]{2,1,0:T(8,128)S(1)} %shard_map.75), channel_id=1, source_target_pairs={{0,24},{8,0},{16,8},{24,16},{1,25},{9,1},{17,9},{25,17},{2,26},{10... | collective-permute-start | bytes 786440 | tf_op jit(solution)/shard_map/ppermute | solution.py:436
